TPU v7x, 32 devices: a whole 2x2x4 slice. The times are simulated.
32 devices in a mesh: group: 2 (over y), seq: 4 (over z), req: 2 (over x), sub: 2 (over core).
Axes of the slice: x: 2, y: 2, z: 4, core: 2. Of those that a mesh axis runs over, the one named last changes fastest.
Arguments:
- latent_codes: bfloat16 [2, 16, 2048, 512], P(None, ('group', 'req', 'sub'), 'seq'), parts along dimension 1, may hold values from -6 to 6
- latent_scales: bfloat16 [2, 16, 2048, 4], P(None, ('group', 'req', 'sub'), 'seq'), parts along dimension 1, may hold values from 0.34 to 3.5
- rope_keys: bfloat16 [2, 16, 2048, 64], P(None, ('group', 'req', 'sub'), 'seq'), parts along dimension 1, may hold values from -6 to 6
- lengths: int32 [16], P(('group', 'req', 'sub')), parts along dimension 0, may hold values from 256 to 2048, as said below
- query_latent: bfloat16 [2, 16, 4, 128, 512], P(None, ('group', 'req', 'sub'), None, 'seq'), parts along dimension 1, may hold values from -64 to 64
- query_rope: bfloat16 [2, 16, 4, 128, 64], P(None, ('group', 'req', 'sub'), None, 'seq'), parts along dimension 1, may hold values from -8 to 8
- new_latent: bfloat16 [2, 16, 4, 512], P(None, ('group', 'req', 'sub')), parts along dimension 1, may hold values from -9 to 9
- new_rope: bfloat16 [2, 16, 4, 64], P(None, ('group', 'req', 'sub')), parts along dimension 1, may hold values from -6 to 6
Outputs:
- attended: bfloat16 [2, 16, 4, 128, 512], P(None, ('group', 'req', 'sub'), None, 'seq'), parts along dimension 1
- cache_codes: bfloat16 [2, 16, 512, 4, 512], P(None, ('group', 'req', 'sub'), None, 'seq'), parts along dimension 1
- cache_scales: bfloat16 [2, 16, 512, 4, 4], P(None, ('group', 'req', 'sub'), None, 'seq'), parts along dimension 1
- cache_rope: bfloat16 [2, 16, 512, 4, 64], P(None, ('group', 'req', 'sub'), None, 'seq'), parts along dimension 1
There are 2 independent parts, one for each index of `group`. A program takes and returns all parts, laid end to end along the dimension named above; each array names one. Nothing has to cross between parts.
Inputs may be any that keep to these rules, and one draw needn't show every extreme that they name: `lengths`: one request is exactly 2048 long.
All inputs are finite; a program needn't handle non-finite values.
Results may differ from a plain program's by a relative error of at most 0.013.
Values may be sent and summed in bfloat16 or wider, within the bound.
A program may use at most 64 MiB of HBM per device.

v0:
```python
import jax
import jax.numpy as jnp
from jax import lax
from jax.sharding import PartitionSpec as P

softmax_gain = 192.0 ** (-0.5)
masked_score = -1e30


def dequantize(code_values, scale_values):
    blocks = scale_values.shape[-1]
    latent_width = code_values.shape[-1]
    shaped = code_values.astype(jnp.float32).reshape(
        code_values.shape[:-1] + (blocks, latent_width // blocks)
    )
    scaled = shaped * scale_values.astype(jnp.float32)[..., None]
    return scaled.reshape(code_values.shape).astype(jnp.bfloat16)


def shard_partial(
    lat_query, rope_query, key_rows, rope_rows, usable, new_keys, new_rope_rows, holds_new
):
    tokens_new, head_count, latent_width = lat_query.shape
    query_rows = lat_query.reshape(tokens_new * head_count, latent_width)
    query_pos = rope_query.reshape(tokens_new * head_count, rope_query.shape[-1])
    scores = jnp.dot(query_rows, key_rows.T, preferred_element_type=jnp.float32)
    scores = (
        scores + jnp.dot(query_pos, rope_rows.T, preferred_element_type=jnp.float32)
    ) * softmax_gain
    fresh_scores = jnp.dot(query_rows, new_keys.T, preferred_element_type=jnp.float32)
    fresh_scores = (
        fresh_scores + jnp.dot(query_pos, new_rope_rows.T, preferred_element_type=jnp.float32)
    ) * softmax_gain
    token_of_row = jnp.arange(tokens_new * head_count, dtype=jnp.int32) // head_count
    causal = (jnp.arange(tokens_new, dtype=jnp.int32)[None, :] <= token_of_row[:, None]) & holds_new
    scores = jnp.where(usable[None, :], scores, masked_score)
    fresh_scores = jnp.where(causal, fresh_scores, masked_score)
    group_peak = jnp.maximum(jnp.max(scores, 1), jnp.max(fresh_scores, 1)).astype(jnp.bfloat16)
    peak_float = group_peak.astype(jnp.float32)[:, None]
    weights = jnp.where(usable[None, :], jnp.exp(scores - peak_float), 0.0).astype(jnp.bfloat16)
    fresh_weights = jnp.where(causal, jnp.exp(fresh_scores - peak_float), 0.0).astype(jnp.bfloat16)
    group_total = jnp.sum(weights.astype(jnp.float32), 1) + jnp.sum(
        fresh_weights.astype(jnp.float32), 1
    )
    group_sum = jnp.dot(weights, key_rows, preferred_element_type=jnp.float32)
    group_sum = group_sum + jnp.dot(fresh_weights, new_keys, preferred_element_type=jnp.float32)
    return (
        group_sum.astype(jnp.bfloat16).reshape(tokens_new, head_count, latent_width),
        group_peak.reshape(tokens_new, head_count),
        group_total.astype(jnp.bfloat16).reshape(tokens_new, head_count),
    )


def merge_groups(pieces):
    group_sum, group_peak, group_total = pieces
    peak_float = group_peak.astype(jnp.float32)
    overall = jnp.max(peak_float, 0)
    factor = jnp.exp(peak_float - overall)
    numerator = jnp.sum(factor[..., None] * group_sum.astype(jnp.float32), 0)
    denominator = jnp.sum(factor * group_total.astype(jnp.float32), 0)
    return (numerator / denominator[..., None]).astype(jnp.bfloat16)


def per_device(
    latent_codes, latent_scales, rope_keys, lengths, query_latent, query_rope, new_latent, new_rope
):
    shard_count = lax.axis_size("seq")
    seq_index = lax.axis_index("seq")
    layer_count, request_count, span, latent_width = latent_codes.shape
    lat_query, rope_query = (
        lax.all_gather(query_latent, "seq", axis=3, tiled=True),
        lax.all_gather(query_rope, "seq", axis=3, tiled=True),
    )

    def regroup_rows(values):
        return values.reshape(
            values.shape[0], values.shape[1], span // shard_count, shard_count, values.shape[-1]
        )

    codes_moved, scales_moved, rope_moved = (
        lax.all_to_all(regroup_rows(latent_codes), "seq", split_axis=3, concat_axis=2, tiled=True),
        lax.all_to_all(regroup_rows(latent_scales), "seq", split_axis=3, concat_axis=2, tiled=True),
        lax.all_to_all(regroup_rows(rope_keys), "seq", split_axis=3, concat_axis=2, tiled=True),
    )
    offsets = jnp.arange(span, dtype=jnp.int32)
    key_rows = dequantize(latent_codes, latent_scales)
    positions = seq_index * span + offsets
    usable = positions[None, :] < lengths[:, None]
    holds_new = seq_index == 0
    per_request = jax.vmap(shard_partial, in_axes=(0, 0, 0, 0, 0, 0, 0, None))
    per_layer = jax.vmap(per_request, in_axes=(0, 0, 0, 0, None, 0, 0, None))
    group_sum, group_peak, group_total = per_layer(
        lat_query, rope_query, key_rows, rope_keys, usable, new_latent, new_rope, holds_new
    )
    attended = merge_groups(
        (
            lax.all_to_all(group_sum[None], "seq", split_axis=4, concat_axis=0, tiled=True),
            lax.all_to_all(group_peak[None], "seq", split_axis=4, concat_axis=0, tiled=True),
            lax.all_to_all(group_total[None], "seq", split_axis=4, concat_axis=0, tiled=True),
        )
    )
    return (attended, codes_moved, scales_moved, rope_moved)


def solution(mesh):
    placed = (
        P(None, ("group", "req", "sub"), "seq", None),
        P(None, ("group", "req", "sub"), "seq", None),
        P(None, ("group", "req", "sub"), "seq", None),
        P(("group", "req", "sub")),
        P(None, ("group", "req", "sub"), None, "seq", None),
        P(None, ("group", "req", "sub"), None, "seq", None),
        P(None, ("group", "req", "sub"), None, None),
        P(None, ("group", "req", "sub"), None, None),
    )
    return jax.shard_map(
        per_device,
        mesh=mesh,
        in_specs=placed,
        out_specs=(
            P(None, ("group", "req", "sub"), None, "seq", None),
            P(None, ("group", "req", "sub"), None, "seq", None),
            P(None, ("group", "req", "sub"), None, "seq", None),
            P(None, ("group", "req", "sub"), None, "seq", None),
        ),
        check_vma=False,
    )
```

profile of v0, /device:TPU:0, one launch (start us, length us, event | category | flops | bytes accessed | tf_op | source)
XLA Modules:
  0.0 215.6 jit_solution(11127280630018597931)
XLA Ops:
  7.9 1.8 reshape.126
  9.8 0.8 copy.66
  10.6 6.3 %all-to-all-start.4 = ((bf16[2,2,128,4,4]{2,4,1,0,3:T(4,128)(2,1)}), bf16[2,2,128,4,4]{2,4,1,0,3:T(4,128)(2,1)S(1)}, u32[]{:S(2)}, u32[]{:S(2)}) async-start(bf16[2,2,128,4,4]{2,4,1,0,3:T(4,128)(2,1)} %copy.66), calls=%async_computation.4 | async-start | bytes 32768 | tf_op jit(solution)/shard_map/all_to_all | solution.py:82
  16.9 1.2 copy.68
  18.1 1.0 copy.69
  19.2 3.4 %all-to-all-done.4 = bf16[2,2,128,4,4]{2,4,1,0,3:T(4,128)(2,1)S(1)} async-done(((bf16[2,2,128,4,4]{2,4,1,0,3:T(4,128)(2,1)}), bf16[2,2,128,4,4]{2,4,1,0,3:T(4,128)(2,1)S(1)}, u32[]{:S(2)}, u32[]{:S(2)}) %all-to-all-start.4) | async-done | bytes 16416 | tf_op jit(solution)/shard_map/all_to_all | solution.py:82
  22.5 3.4 %all-to-all-start.5 = ((bf16[2,2,128,4,64]{2,4,1,0,3:T(8,128)(2,1)}), bf16[2,2,128,4,64]{2,4,1,0,3:T(8,128)(2,1)S(1)}, u32[]{:S(2)}, u32[]{:S(2)}) async-start(bf16[2,2,128,4,64]{2,4,1,0,3:T(8,128)(2,1)} %copy.69), calls=%async_computation.5 | async-start | bytes 524288 | tf_op jit(solution)/shard_map/all_to_all | solution.py:83
  25.9 1.0 copy.57
  26.9 3.9 %mul.38 = f32[2,2,512,4,128]{4,3,2,1,0:T(4,128)} broadcast(f32[2,2,512,4]{3,2,1,0:T(8,128)S(1)} %copy.57), dimensions={0,1,2,3} | broadcast | bytes 4227072 | tf_op jit(solution)/shard_map/mul | solution.py:16
  30.8 5.6 %mul.39 = f32[2,2,512,512]{3,2,1,0:T(8,128)} reshape(f32[2,2,512,4,128]{4,3,2,1,0:T(4,128)} %mul.38) | data formatting | bytes 8388608 | tf_op jit(solution)/shard_map/mul | solution.py:16
  36.4 2.2 %copy.63 = bf16[2,2,512,512]{3,1,2,0:T(2,128)(2,1)S(1)} copy(bf16[2,2,512,512]{3,2,1,0:T(8,128)(2,1)S(1)} %copy-done.2) | data formatting | bytes 4194304 | tf_op args[0]
  38.6 2.0 copy.64
  40.6 1.7 all-to-all-done.5
  42.3 4.5 %all-to-all-start.3 = ((bf16[2,2,128,4,512]{4,2,1,0,3:T(8,128)(2,1)}), bf16[2,2,128,4,512]{4,2,1,0,3:T(8,128)(2,1)}, u32[]{:S(2)}, u32[]{:S(2)}) async-start(bf16[2,2,128,4,512]{4,2,1,0,3:T(8,128)(2,1)} %copy.64), calls=%async_computation.3 | async-start | bytes 4194304 | tf_op jit(solution)/shard_map/all_to_all | solution.py:81
  46.8 71.2 %all_gather.7 = bf16[2,2,4,128,64]{4,3,2,1,0:T(8,128)(2,1)S(1)} all-gather(bf16[2,2,4,32,64]{4,3,2,1,0:T(8,128)(2,1)S(1)} %copy-done.4), channel_id=1, replica_groups=mesh['group'=2,'seq'=4,'req'=2,'sub'=2] {'seq'}, dimensions={3}, use_global_device_ids=true | all-gather | bytes 327680 | tf_op jit(solution)/shard_map/all_gather | solution.py:72
  118.3 2.8 %fusion.16 = f32[2,2,512,512]{2,3,1,0:T(8,128)} fusion(bf16[2,2,512,64]{3,2,1,0:T(8,128)(2,1)S(1)} %bitcast.77, bf16[2,2,512,64]{2,3,1,0:T(8,128)(2,1)S(1)} %copy-done.3), kind=kOutput, calls=%fused_computation.39 | convolution fusion | flops 134217728 | bytes 4718592 | tf_op jit(solution)/shard_map/vmap(vmap())/dot_general | solution.py:28
  121.1 2.3 %fusion.15 = (bf16[2,2,512]{2,1,0:T(2,128)(2,1)S(1)}, f32[2,2,512,4]{2,3,1,0:T(4,128)S(1)}) fusion(f32[2,2,512,4]{2,3,1,0:T(4,128)S(1)} %fusion.17, bf16[2,2,512,512]{3,2,1,0:T(8,128)(2,1)} %bitcast.74, bf16[2,2,4,512]{3,2,1,0:T(4,128)(2,1)S(1)} %copy-done, pred[512,4]{0,1:T(4,128)(4,1)S(1)} %fusion.8), kind=kOutput, calls=%fused_computation.38 | convolution fusion | flops 8419328 | bytes 2185216 | tf_op jit(solution)/shard_map/vmap(vmap())/dot_general | solution.py:30
  123.4 5.6 %fusion.14 = (bf16[2,2,512]{2,1,0:T(2,128)(2,1)S(1)}, f32[2,2,512,512]{2,3,1,0:T(8,128)S(1)}) fusion(f32[2,2,512,512]{2,3,1,0:T(8,128)} %fusion.16, bf16[2,2,512,512]{3,2,1,0:T(8,128)(2,1)} %bitcast.75, f32[2,2,512,512]{3,2,1,0:T(8,128)} %mul.39, bf16[2,2,512,512]{3,2,1,0:T(8,128)(2,1)S(1)} %copy-done.2, pred[2,512]{1,0:T(4,128)(4,1)S(1)} %broadcast_compare_fusion), kind=kOutput, calls=%fused_computation.37 | convolution fusion | flops 1081079808 | bytes 16782336 | tf_op jit(solution)/shard_map/vmap(vmap())/dot_general | solution.py:26
  129.0 1.9 copy-done.1
  131.9 0.8 reshape.135
  132.7 5.0 %all-to-all-start.2 = ((bf16[4,2,256]{2,1,0:T(2,128)(2,1)}), bf16[4,2,256]{2,1,0:T(2,128)(2,1)S(1)}, u32[]{:S(2)}, u32[]{:S(2)}) async-start(bf16[4,2,256]{2,1,0:T(2,128)(2,1)} %reshape.135), calls=%async_computation.2 | async-start | bytes 8192 | tf_op jit(solution)/shard_map/all_to_all | solution.py:99
  137.6 7.1 %fusion.5 = f32[2,2,512,512]{3,2,1,0:T(8,128)} fusion(f32[2,2,512,512]{2,3,1,0:T(8,128)} %copy-done.1, f32[2,2,512]{2,1,0:T(2,128)S(1)} %get-tuple-element.20, pred[2,512]{1,0:T(4,128)(4,1)S(1)} %broadcast_compare_fusion, f32[2,2,512,512]{3,2,1,0:T(8,128)} %mul.39, bf16[2,2,512,512]{3,2,1,0:T(8,128)(2,1)S(1)} %copy-done.2), kind=kOutput, calls=%fused_computation.13 | convolution fusion | flops 1080033280 | bytes 14689280 | tf_op jit(solution)/shard_map/vmap(vmap())/dot_general | solution.py:45
  145.0 0.8 reshape.133
  145.7 5.1 %all-to-all-start = ((bf16[4,2,256]{2,1,0:T(2,128)(2,1)}), bf16[4,2,256]{2,1,0:T(2,128)(2,1)S(1)}, u32[]{:S(2)}, u32[]{:S(2)}) async-start(bf16[4,2,256]{2,1,0:T(2,128)(2,1)} %reshape.133), calls=%async_computation | async-start | bytes 8192 | tf_op jit(solution)/shard_map/all_to_all | solution.py:98
  150.8 3.0 %add_convert_fusion = bf16[2,2,512,512]{3,2,1,0:T(8,128)(2,1)S(1)} fusion(f32[2,2,512,512]{3,2,1,0:T(8,128)} %fusion.5, bf16[2,2,4,512]{3,2,1,0:T(4,128)(2,1)S(1)} %copy-done, f32[2,2,512,4]{2,3,1,0:T(4,128)S(1)} %get-tuple-element.27, f32[2,2,512]{2,1,0:T(2,128)S(1)} %get-tuple-element.20, pred[512,4]{0,1:T(4,128)(4,1)S(1)} %fusion.8), kind=kOutput, calls=%fused_computation.6 | convolution fusion | flops 10510336 | bytes 6350848 | tf_op jit(solution)/shard_map/vmap(vmap())/dot_general | solution.py:46
  153.8 3.0 %copy.61 = bf16[1,2,2,4,128,512]{5,3,2,1,0,4:T(4,128)(2,1)} copy(bf16[1,2,2,4,128,512]{5,4,3,2,1,0:T(8,128)(2,1)S(1)} %bitcast.72) | data formatting | bytes 4194304 | tf_op jit(solution)/shard_map/broadcast_in_dim;vmap(vmap())/reshape | solution.py:97
  156.8 5.1 %all-to-all-start.1 = ((bf16[1,2,2,4,128,512]{5,3,2,1,0,4:T(4,128)(2,1)}), bf16[1,2,2,4,128,512]{5,3,2,1,0,4:T(4,128)(2,1)S(1)}, u32[]{:S(2)}, u32[]{:S(2)}) async-start(bf16[1,2,2,4,128,512]{5,3,2,1,0,4:T(4,128)(2,1)} %copy.61), calls=%async_computation.1 | async-start | bytes 4194304 | tf_op jit(solution)/shard_map/all_to_all | solution.py:97
  162.5 0.7 bitcast_bitcast_fusion
  163.2 3.1 %copy.65 = bf16[2,2,128,4,512]{4,2,3,1,0:T(8,128)(2,1)} copy(bf16[2,2,128,4,512]{4,2,1,0,3:T(8,128)(2,1)} %all-to-all-done.3) | data formatting | bytes 4194304 | tf_op jit(solution)/shard_map/all_to_all | solution.py:81
  167.4 38.4 %all-to-all-done.1 = bf16[1,2,2,4,128,512]{5,3,2,1,0,4:T(4,128)(2,1)S(1)} async-done(((bf16[1,2,2,4,128,512]{5,3,2,1,0,4:T(4,128)(2,1)}), bf16[1,2,2,4,128,512]{5,3,2,1,0,4:T(4,128)(2,1)S(1)}, u32[]{:S(2)}, u32[]{:S(2)}) %all-to-all-start.1) | async-done | bytes 2097184 | tf_op jit(solution)/shard_map/all_to_all | solution.py:97
  205.9 1.5 fusion
  207.7 1.1 copy.71
  (39 shorter events, 4.2 us)
Async XLA Ops:
  7.2 113.9 %copy-start = (bf16[2,2,4,512]{3,2,1,0:T(4,128)(2,1)S(1)}, bf16[2,2,4,512]{3,2,1,0:T(4,128)(2,1)}, u32[]{:S(2)}) copy-start(bf16[2,2,4,512]{3,2,1,0:T(4,128)(2,1)} %param.14) | copy-start | bytes 49156
  7.2 113.9 %all-gather.2.cloned.1.call-start = ((), (), s32[]{:S(2)}) async-start(), calls=%async_computation.6 | async-start | bytes 2621440 | tf_op jit(solution)/shard_map/all_gather | solution.py:71
  10.6 11.9 %all-to-all-start.4 = ((bf16[2,2,128,4,4]{2,4,1,0,3:T(4,128)(2,1)}), bf16[2,2,128,4,4]{2,4,1,0,3:T(4,128)(2,1)S(1)}, u32[]{:S(2)}, u32[]{:S(2)}) async-start(bf16[2,2,128,4,4]{2,4,1,0,3:T(4,128)(2,1)} %copy.66), calls=%async_computation.4 | async-start | bytes 32768 | tf_op jit(solution)/shard_map/all_to_all | solution.py:82
  22.5 19.8 %all-to-all-start.5 = ((bf16[2,2,128,4,64]{2,4,1,0,3:T(8,128)(2,1)}), bf16[2,2,128,4,64]{2,4,1,0,3:T(8,128)(2,1)S(1)}, u32[]{:S(2)}, u32[]{:S(2)}) async-start(bf16[2,2,128,4,64]{2,4,1,0,3:T(8,128)(2,1)} %copy.69), calls=%async_computation.5 | async-start | bytes 524288 | tf_op jit(solution)/shard_map/all_to_all | solution.py:83
  30.8 5.6 %copy-start.2 = (bf16[2,2,512,512]{3,2,1,0:T(8,128)(2,1)S(1)}, bf16[2,2,512,512]{3,2,1,0:T(8,128)(2,1)}, u32[]{:S(2)}) copy-start(bf16[2,2,512,512]{3,2,1,0:T(8,128)(2,1)} %param.8) | copy-start | bytes 6291460
  38.6 8.2 %copy-start.4 = (bf16[2,2,4,32,64]{4,3,2,1,0:T(8,128)(2,1)S(1)}, bf16[2,2,4,32,64]{4,3,2,1,0:T(8,128)(2,1)}, u32[]{:S(2)}) copy-start(bf16[2,2,4,32,64]{4,3,2,1,0:T(8,128)(2,1)} %param.13) | copy-start | bytes 196612
  38.6 79.4 %copy-start.6 = (s32[2]{0:T(128)S(1)}, s32[2]{0:T(128)}, u32[]{:S(2)}) copy-start(s32[2]{0:T(128)} %param.11) | copy-start | bytes 28
  38.6 79.5 %copy-start.5 = (bf16[2,2,4,64]{3,2,1,0:T(4,128)(2,1)S(1)}, bf16[2,2,4,64]{3,2,1,0:T(4,128)(2,1)}, u32[]{:S(2)}) copy-start(bf16[2,2,4,64]{3,2,1,0:T(4,128)(2,1)} %param.15) | copy-start | bytes 6148
  38.6 79.7 %copy-start.3 = (bf16[2,2,512,64]{2,3,1,0:T(8,128)(2,1)S(1)}, bf16[2,2,512,64]{2,3,1,0:T(8,128)(2,1)}, u32[]{:S(2)}) copy-start(bf16[2,2,512,64]{2,3,1,0:T(8,128)(2,1)} %param.10) | copy-start | bytes 786436
  42.3 90.3 %all-to-all-start.3 = ((bf16[2,2,128,4,512]{4,2,1,0,3:T(8,128)(2,1)}), bf16[2,2,128,4,512]{4,2,1,0,3:T(8,128)(2,1)}, u32[]{:S(2)}, u32[]{:S(2)}) async-start(bf16[2,2,128,4,512]{4,2,1,0,3:T(8,128)(2,1)} %copy.64), calls=%async_computation.3 | async-start | bytes 4194304 | tf_op jit(solution)/shard_map/all_to_all | solution.py:81
  128.9 2.0 copy-start.1
  132.7 13.1 %all-to-all-start.2 = ((bf16[4,2,256]{2,1,0:T(2,128)(2,1)}), bf16[4,2,256]{2,1,0:T(2,128)(2,1)S(1)}, u32[]{:S(2)}, u32[]{:S(2)}) async-start(bf16[4,2,256]{2,1,0:T(2,128)(2,1)} %reshape.135), calls=%async_computation.2 | async-start | bytes 8192 | tf_op jit(solution)/shard_map/all_to_all | solution.py:99
  145.7 11.0 %all-to-all-start = ((bf16[4,2,256]{2,1,0:T(2,128)(2,1)}), bf16[4,2,256]{2,1,0:T(2,128)(2,1)S(1)}, u32[]{:S(2)}, u32[]{:S(2)}) async-start(bf16[4,2,256]{2,1,0:T(2,128)(2,1)} %reshape.133), calls=%async_computation | async-start | bytes 8192 | tf_op jit(solution)/shard_map/all_to_all | solution.py:98
  156.8 49.1 %all-to-all-start.1 = ((bf16[1,2,2,4,128,512]{5,3,2,1,0,4:T(4,128)(2,1)}), bf16[1,2,2,4,128,512]{5,3,2,1,0,4:T(4,128)(2,1)S(1)}, u32[]{:S(2)}, u32[]{:S(2)}) async-start(bf16[1,2,2,4,128,512]{5,3,2,1,0,4:T(4,128)(2,1)} %copy.61), calls=%async_computation.1 | async-start | bytes 4194304 | tf_op jit(solution)/shard_map/all_to_all | solution.py:97
Sparse Core Ops, SparseCore 0:
  9.6 73.4 all-gather.1
where the time goes:
time: 216 us
  blocking collectives  71.2 us (33%)
  waiting for transfers between devices  44.2 us (20%)
  local copies, waits for them, and re-layouts  32.4 us (15%)
  starting transfers between devices  29.4 us (14%)
  matrix products  20.9 us (10%)
  between operations  14.3 us (7%)
  other arithmetic  3.24 us (2%)
    all_gather x1, blocking collectives, per_device(): lax.all_gather(query_rope, 'seq', axis=3, tiled=True)  71.2 us
    all_to_all x1, waiting for transfers between devices, per_device(): lax.all_to_all(group_sum[None], 'seq', split_axis=4, concat_axis=0, tiled...  38.4 us
    mul x2, local copies, waits for them, and re-layouts, dequantize(): scaled = shaped * scale_values.astype(jnp.float32)[..., None]  9.47 us
    unnamed x22, local copies, waits for them, and re-layouts  9.29 us
    dot_general x1, matrix products, shard_partial(): group_sum = jnp.dot(weights, key_rows, preferred_element_type=jnp.float32)  7.14 us
    all_to_all x1, starting transfers between devices, per_device(): lax.all_to_all(regroup_rows(latent_scales), 'seq', split_axis=3, concat_a...  6.32 us
    reshape x4, local copies, waits for them, and re-layouts, regroup_rows(): values.reshape(values.shape[0], values.shape[1], span // shard_count, sha...  5.68 us
    dot_general x1, matrix products, shard_partial(): scores = jnp.dot(query_rows, key_rows.T, preferred_element_type=jnp.float32)  5.57 us
  transfers between devices with their start and end apart: 7, of which 3 were waited for; matrix products, arithmetic and copies ran while one was open for 24% of the time, Pallas kernels for 0%

commit v1 on v0

--- a/solution.py
+++ b/solution.py
@@ -1,6 +1,8 @@
 import jax
 import jax.numpy as jnp
 from jax import lax
+from jax.experimental import pallas as pl
+from jax.experimental.pallas import tpu as pltpu
 from jax.sharding import PartitionSpec as P
 
 softmax_gain = 192.0 ** (-0.5)
@@ -102,6 +104,293 @@
     return (attended, codes_moved, scales_moved, rope_moved)
 
 
+AUX = 80
+
+
+def _relay_kernel(
+    len_ref, codes_ref, aux_ref, q_ref, qr_ref, new_ref, newr_ref,
+    att_ref, cache_ref, caux_ref,
+    kbuf, abuf, qbuf, qrbuf, nkbuf, nrbuf, result, acc, peak, total,
+    load_sem, out_sem, send_sem, recv_sem, q_send, q_recv, f_send, f_recv, r_send, r_recv,
+):
+    pairs, groups, rows, width = codes_ref.shape
+    span = groups * rows
+    half = q_ref.shape[1]
+    rope = qr_ref.shape[2]
+    heads = half // new_ref.shape[1]
+    fresh = new_ref.shape[1]
+    me = lax.axis_index("seq")
+    inner = (me == 1) | (me == 2)
+    outer = (me - 1) * 3
+    across = 3 - me
+    hub = 1 + me // 3
+
+    def neighbour_signal(target):
+        pl.semaphore_signal(
+            pltpu.get_barrier_semaphore(), inc=1, device_id={"seq": target},
+            device_id_type=pl.DeviceIdType.MESH,
+        )
+
+    loads = [
+        pltpu.make_async_copy(codes_ref, kbuf.at[0], load_sem.at[0]),
+        pltpu.make_async_copy(aux_ref, abuf.at[0], load_sem.at[1]),
+        pltpu.make_async_copy(q_ref, qbuf.at[:, 0], load_sem.at[2]),
+        pltpu.make_async_copy(qr_ref, qrbuf.at[:, 0], load_sem.at[3]),
+    ]
+    for load in loads:
+        load.start()
+
+    @pl.when(inner)
+    def _():
+        neighbour_signal(outer)
+        neighbour_signal(across)
+        pl.semaphore_wait(pltpu.get_barrier_semaphore(), 2)
+
+    @pl.when(jnp.logical_not(inner))
+    def _():
+        neighbour_signal(hub)
+        pl.semaphore_wait(pltpu.get_barrier_semaphore(), 1)
+
+    def remote(src, dst, send, recv, target):
+        return pltpu.make_async_remote_copy(
+            src_ref=src, dst_ref=dst, send_sem=send, recv_sem=recv,
+            device_id={"seq": target}, device_id_type=pl.DeviceIdType.MESH,
+        )
+
+    def shard(src_slot, dst_slot, c, target):
+        return (
+            remote(kbuf.at[src_slot, c], kbuf.at[dst_slot, c],
+                   send_sem.at[0, dst_slot, c], recv_sem.at[0, dst_slot, c], target),
+            remote(abuf.at[src_slot, c], abuf.at[dst_slot, c],
+                   send_sem.at[1, dst_slot, c], recv_sem.at[1, dst_slot, c], target),
+        )
+
+    def queries(c, target):
+        return (
+            remote(qbuf.at[c, 0], qbuf.at[c, 1], q_send.at[0, c], q_recv.at[0, c], target),
+            remote(qrbuf.at[c, 0], qrbuf.at[c, 1], q_send.at[1, c], q_recv.at[1, c], target),
+        )
+
+    def shard_of(slot, own, partner):
+        base = own + (slot % 2) * (partner - own)
+        return base + (slot // 2) * (3 - 2 * base)
+
+    def handover(slot, c, group, place, target):
+        return (
+            remote(kbuf.at[slot, c, group], cache_ref.at[c, place],
+                   f_send.at[0, slot, c], f_recv.at[0, slot, c], target),
+            remote(abuf.at[slot, c, group], caux_ref.at[c, place],
+                   f_send.at[1, slot, c], f_recv.at[1, slot, c], target),
+        )
+
+    def keep(slot, c, place):
+        return (
+            pltpu.make_async_copy(kbuf.at[slot, c, me], cache_ref.at[c, place], out_sem.at[0, slot, c]),
+            pltpu.make_async_copy(abuf.at[slot, c, me], caux_ref.at[c, place], out_sem.at[1, slot, c]),
+        )
+
+    def results(c, target):
+        return remote(result.at[c], att_ref.at[c], r_send.at[c], r_recv.at[c], target)
+
+    def start(copies):
+        for copy in copies:
+            copy.start()
+
+    for load in loads:
+        load.wait()
+
+    @pl.when(jnp.logical_not(inner))
+    def _():
+        @pl.loop(0, pairs)
+        def _(c):
+            copies = shard(0, 1, c, hub) + queries(c, hub)
+            start(copies)
+            start(keep(0, c, me))
+            for copy in copies:
+                copy.wait_send()
+
+        @pl.loop(0, pairs)
+        def _(c):
+            for slot in (0, 2, 3):
+                for copy in handover(slot, c, me, shard_of(slot, hub, me), hub):
+                    copy.wait_recv()
+            results(c, hub).wait_recv()
+            for copy in keep(0, c, me):
+                copy.wait()
+
+    @pl.when(inner)
+    def _():
+        start(shard(0, 2, 0, across))
+        start(shard(0, 2, 1, across))
+
+        @pl.loop(0, pairs)
+        def _(c):
+            start(handover(0, c, outer, me, outer))
+            start(keep(0, c, me))
+            nkbuf[c] = jnp.zeros(nkbuf.shape[1:], nkbuf.dtype)
+            nrbuf[c] = jnp.zeros(nrbuf.shape[1:], nrbuf.dtype)
+            nkbuf[c, 0:fresh, :] = new_ref[c]
+            nrbuf[c, 0:fresh, :] = newr_ref[c]
+
+        def relay(c):
+            for copy in shard(0, 1, c, outer):
+                copy.wait_recv()
+            start(shard(1, 3, c, across))
+            start(keep(1, c, outer))
+
+        relay(0)
+        start(shard(0, 2, 2, across))
+
+        @pl.loop(0, pairs)
+        def _(c):
+            @pl.when(c + 1 < pairs)
+            def _():
+                relay(c + 1)
+
+            @pl.when(c + 3 < pairs)
+            def _():
+                start(shard(0, 2, c + 3, across))
+
+            for copy in queries(c, outer):
+                copy.wait_recv()
+            q = qbuf[c].reshape(2 * half, width)
+            qr = qrbuf[c].reshape(2 * half, rope)
+            dims = (((1,), (1,)), ((), ()))
+            s = lax.dot_general(q, nkbuf[c], dims, preferred_element_type=jnp.float32)
+            s = s + lax.dot_general(qr, nrbuf[c], dims, preferred_element_type=jnp.float32)
+            s = s * softmax_gain
+            token = (lax.broadcasted_iota(jnp.int32, s.shape, 0) % half) // heads
+            s = jnp.where(lax.broadcasted_iota(jnp.int32, s.shape, 1) <= token, s, masked_score)
+            m = jnp.max(s, axis=1, keepdims=True)
+            w = jnp.exp(s - m).astype(jnp.bfloat16)
+            peak[...] = jnp.broadcast_to(m, peak.shape)
+            total[...] = jnp.broadcast_to(
+                jnp.sum(w.astype(jnp.float32), axis=1, keepdims=True), total.shape
+            )
+            acc[...] = jnp.dot(w, nkbuf[c], preferred_element_type=jnp.float32)
+            length = len_ref[c % len_ref.shape[0]]
+
+            @pl.loop(0, 4)
+            def _(slot):
+                place = shard_of(slot, me, outer)
+
+                @pl.when(slot >= 2)
+                def _():
+                    for copy in shard(0, slot, c, across):
+                        copy.wait_recv()
+                    start(handover(slot, c, outer, place, outer))
+                    start(keep(slot, c, place))
+
+                keys, ropes = [], []
+                for k in range(groups):
+                    scales = abuf[slot, c, k, rope:AUX, :].astype(jnp.float32).T
+                    codes = kbuf[slot, c, k].astype(jnp.float32)
+                    blocks = [
+                        codes[:, b * 128:(b + 1) * 128] * scales[:, b:b + 1]
+                        for b in range(width // 128)
+                    ]
+                    keys.append(jnp.concatenate(blocks, axis=1).astype(jnp.bfloat16))
+                    ropes.append(abuf[slot, c, k, 0:rope, :])
+                keys = jnp.concatenate(keys, axis=0)
+                q = qbuf[c].reshape(2 * half, width)
+                qr = qrbuf[c].reshape(2 * half, rope)
+                s = lax.dot_general(q, keys, dims, preferred_element_type=jnp.float32)
+                s = s + jnp.dot(qr, jnp.concatenate(ropes, axis=1), preferred_element_type=jnp.float32)
+                s = s * softmax_gain
+                column = lax.broadcasted_iota(jnp.int32, (1, span), 1)
+                position = place * span + (column % rows) * groups + column // rows
+                s = jnp.where(position < length, s, masked_score)
+                before = peak[:, 0:1]
+                m = jnp.maximum(before, jnp.max(s, axis=1, keepdims=True))
+                factor = jnp.exp(before - m)
+                w = jnp.exp(s - m).astype(jnp.bfloat16)
+                peak[...] = jnp.broadcast_to(m, peak.shape)
+                total[...] = factor * total[...] + jnp.sum(w.astype(jnp.float32), axis=1, keepdims=True)
+                acc[...] = factor * acc[...] + jnp.dot(w, keys, preferred_element_type=jnp.float32)
+
+            done = (acc[...] / total[:, 0:1]).astype(jnp.bfloat16)
+            result[c] = done[half:]
+            results(c, outer).start()
+            att_ref[c] = done[:half]
+
+        @pl.loop(0, pairs)
+        def _(c):
+            for copy in shard(0, 2, c, across) + shard(1, 3, c, across):
+                copy.wait_send()
+            for slot in (0, 2, 3):
+                for copy in handover(slot, c, outer, shard_of(slot, me, outer), outer):
+                    copy.wait_send()
+            for slot in range(4):
+                for copy in keep(slot, c, shard_of(slot, me, outer)):
+                    copy.wait()
+            results(c, outer).wait_send()
+
+
+def per_device_line(
+    latent_codes, latent_scales, rope_keys, lengths, query_latent, query_rope, new_latent, new_rope
+):
+    groups = 4
+    layers, requests, span, width = latent_codes.shape
+    pairs, rows = layers * requests, span // groups
+    rope, blocks = rope_keys.shape[-1], latent_scales.shape[-1]
+    tokens, heads = query_latent.shape[2:4]
+    half = tokens * heads
+    codes = latent_codes.reshape(pairs, rows, groups, width).transpose(0, 2, 1, 3)
+    ropes = rope_keys.reshape(pairs, rows, groups, rope).transpose(0, 2, 3, 1)
+    scales = latent_scales.reshape(pairs, rows, groups, blocks).transpose(0, 2, 3, 1)
+    aux = jnp.concatenate(
+        [ropes, scales, jnp.zeros((pairs, groups, AUX - rope - blocks, rows), jnp.bfloat16)], axis=2
+    )
+    any_spec = pl.BlockSpec(memory_space=pl.ANY)
+    vmem_spec = pl.BlockSpec(memory_space=pltpu.VMEM)
+    dma = pltpu.SemaphoreType.DMA
+    bf16, f32 = jnp.bfloat16, jnp.float32
+    att, cache, caux = pl.pallas_call(
+        _relay_kernel,
+        out_shape=(
+            jax.ShapeDtypeStruct((pairs, half, width), bf16),
+            jax.ShapeDtypeStruct((pairs, groups, rows, width), bf16),
+            jax.ShapeDtypeStruct((pairs, groups, AUX, rows), bf16),
+        ),
+        in_specs=[pl.BlockSpec(memory_space=pltpu.SMEM), any_spec, any_spec, any_spec, any_spec,
+                  vmem_spec, vmem_spec],
+        out_specs=(vmem_spec, any_spec, any_spec),
+        scratch_shapes=[
+            pltpu.VMEM((4, pairs, groups, rows, width), bf16),
+            pltpu.VMEM((4, pairs, groups, AUX, rows), bf16),
+            pltpu.VMEM((pairs, 2, half, width), bf16),
+            pltpu.VMEM((pairs, 2, half, rope), bf16),
+            pltpu.VMEM((pairs, 128, width), bf16),
+            pltpu.VMEM((pairs, 128, rope), bf16),
+            pltpu.VMEM((pairs, half, width), bf16),
+            pltpu.VMEM((2 * half, width), f32),
+            pltpu.VMEM((2 * half, 128), f32),
+            pltpu.VMEM((2 * half, 128), f32),
+            dma((4,)), dma((2, 4, pairs)), dma((2, 4, pairs)), dma((2, 4, pairs)),
+            dma((2, pairs)), dma((2, pairs)), dma((2, 4, pairs)), dma((2, 4, pairs)),
+            dma((pairs,)), dma((pairs,)),
+        ],
+        compiler_params=pltpu.CompilerParams(
+            collective_id=0, has_side_effects=True, vmem_limit_bytes=40 << 20
+        ),
+    )(
+        lengths, codes, aux,
+        query_latent.reshape(pairs, half, width), query_rope.reshape(pairs, half, rope),
+        new_latent.reshape(pairs, tokens, width), new_rope.reshape(pairs, tokens, rope),
+    )
+    spread = caux.reshape(layers, requests, groups, AUX, rows)
+
+    def as_cache(values):
+        return values.transpose(0, 1, 2, 4, 3).reshape(layers, requests, span, 1, values.shape[3])
+
+    return (
+        att.reshape(query_latent.shape),
+        cache.reshape(layers, requests, span, 1, width),
+        as_cache(spread[:, :, :, rope:rope + blocks]),
+        as_cache(spread[:, :, :, :rope]),
+    )
+
+
 def solution(mesh):
     placed = (
         P(None, ("group", "req", "sub"), "seq", None),
@@ -114,7 +403,7 @@
         P(None, ("group", "req", "sub"), None, None),
     )
     return jax.shard_map(
-        per_device,
+        per_device_line if mesh.shape["seq"] == 4 else per_device,
         mesh=mesh,
         in_specs=placed,
         out_specs=(

time: 216 us -> 131 us (0.61)
  Pallas kernels: 0 us -> 119 us
  blocking collectives: 71.2 us -> 0 us
  waiting for transfers between devices: 44.2 us -> 0 us
  starting transfers between devices: 29.4 us -> 0 us
  local copies, waits for them, and re-layouts: 32.4 us -> 11 us
  matrix products: 20.9 us -> 0 us
  between operations: 14.3 us -> 0.75 us
  other arithmetic: 3.24 us -> 0.13 us
    pallas_call x0 -> x1, Pallas kernels: none -> 119 us  [per_device_line(): pl.pallas_call(_relay_kernel, out_shape=(jax.ShapeDtypeStruct((pairs, hal...]
    all_gather x1 -> x0, blocking collectives: 71.2 us -> none  [per_device(): lax.all_gather(query_rope, 'seq', axis=3, tiled=True)]
    all_to_all x6 -> x0, waiting for transfers between devices: 43.5 us -> none  [the longest x1 38.4 us: per_device(): lax.all_to_all(group_sum[None], 'seq', split_axis=4, concat_axis=0, tiled...]
    all_to_all x6 -> x0, starting transfers between devices: 29.3 us -> none  [the longest x1 6.32 us: per_device(): lax.all_to_all(regroup_rows(latent_scales), 'seq', split_axis=3, concat_a...]
    dot_general x6 -> x0, matrix products: 20.9 us -> none  [the longest x1 7.14 us: shard_partial(): group_sum = jnp.dot(weights, key_rows, preferred_element_type=jnp.float32)]
    mul x2 -> x0, local copies, waits for them, and re-layouts: 9.47 us -> none  [dequantize(): scaled = shaped * scale_values.astype(jnp.float32)[..., None]]
    unnamed x22 -> x13, local copies, waits for them, and re-layouts: 9.29 us -> 3.91 us
    all_to_all x2 -> x0, local copies, waits for them, and re-layouts: 3.71 us -> none  [the longest x1 3.09 us: per_device(): lax.all_to_all(regroup_rows(latent_codes), 'seq', split_axis=3, concat_ax...]
  transfers between devices with their start and end apart: 7 -> 0, of which waited for: 3 -> 0; matrix products, arithmetic and copies ran while one was open for 24% -> 0% of each run, Pallas kernels for 0% -> 0%
where the time goes in v1:
time: 131 us
  Pallas kernels  119 us (91%)
  local copies, waits for them, and re-layouts  11 us (8%)
    pallas_call x1, Pallas kernels, per_device_line(): pl.pallas_call(_relay_kernel, out_shape=(jax.ShapeDtypeStruct((pairs, hal...  119 us
    unnamed x13, local copies, waits for them, and re-layouts  3.91 us
    reshape x2, local copies, waits for them, and re-layouts, per_device_line(): latent_codes.reshape(pairs, rows, groups, width).transpose(0, 2, 1, 3)  3.01 us

profile of v1, /device:TPU:0, one launch (start us, length us, event | category | flops | bytes accessed | tf_op | source)
XLA Modules:
  0.0 130.8 jit_solution(15470513320810734463)
XLA Ops:
  0.6 0.1 pad.2.clone
  0.7 1.8 %reshape.46 = bf16[4,128,4,4]{2,1,3,0:T(8,128)(2,1)S(1)} reshape(bf16[2,2,512,4]{2,3,1,0:T(4,128)(2,1)} %param.9) | data formatting | bytes 32768 | tf_op jit(solution)/shard_map/reshape | solution.py:340
  2.6 0.2 copy.18
  2.8 1.2 copy.16
  4.0 0.3 copy.17
  4.3 0.1 maximum_maximum_fusion.aux_ref
  4.4 2.6 %reshape.44 = bf16[4,128,4,512]{3,2,1,0:T(4,128)(2,1)S(1)} reshape(bf16[2,2,512,512]{3,2,1,0:T(8,128)(2,1)} %param.8) | data formatting | bytes 4194304 | tf_op jit(solution)/shard_map/reshape | solution.py:338
  7.0 0.0 copy-start
  7.0 0.0 copy-start.1
  7.0 0.0 copy-start.2
  7.0 0.0 copy-start.3
  7.1 0.0 copy-start.4
  7.1 0.5 copy.23
  7.5 0.5 copy-done
  8.0 0.0 copy-done.1
  8.1 0.0 copy-done.2
  8.1 0.0 copy-done.3
  8.1 0.0 copy-done.4
  8.1 119.0 %shard_map.111 = (bf16[4,128,512]{2,1,0:T(8,128)(2,1)S(1)}, bf16[4,4,128,512]{3,2,1,0:T(8,128)(2,1)S(1)}, bf16[4,4,80,128]{3,2,1,0:T(8,128)(2,1)S(1)}) custom-call(s32[2]{0:T(128)S(1)} %copy-done.4, bf16[4,4,128,512]{3,2,1,0:T(8,128)(2,1)S(1)} %bitcast.27, bf16[4,4,80,128]{3,2,1,0:T(8,128)(2,1)S(1)} %maximum_maximum_fusion.aux_ref, ...), custom_call_target="tpu_custom_call" | custom-call | tf_op jit(solution)/shard_map/pallas_call | solution.py:348
  127.1 0.6 slice_bitcast_fusion.1
  127.7 0.2 copy.20
  127.9 0.8 reshape.55
  128.7 0.8 copy.26
  129.5 1.3 %copy.27 = bf16[2,2,512,1,512]{4,2,3,1,0:T(8,128)(2,1)} copy(bf16[2,2,512,1,512]{4,2,3,1,0:T(8,128)(2,1)S(1)} %bitcast.28) | data formatting | bytes 4194304
  (2 shorter events, 0.0 us)
Async XLA Ops:
  7.0 1.0 copy-start
  7.0 1.1 copy-start.1
  7.0 1.0 copy-start.2
  7.0 1.0 copy-start.3
  7.1 1.0 copy-start.4

commit v2 on v1

--- a/solution.py
+++ b/solution.py
@@ -104,26 +104,27 @@
     return (attended, codes_moved, scales_moved, rope_moved)
 
 
-AUX = 80
-
-
 def _relay_kernel(
-    len_ref, codes_ref, aux_ref, q_ref, qr_ref, new_ref, newr_ref,
-    att_ref, cache_ref, caux_ref,
-    kbuf, abuf, qbuf, qrbuf, nkbuf, nrbuf, result, acc, peak, total,
+    len_ref, codes_ref, rope_ref, scale_ref, q_ref, qr_ref, new_ref, newr_ref,
+    att_ref, cache_ref, crope_ref, cscale_ref,
+    kbuf, abuf, raw, rawr, raws, stage, turned, qbuf, qrbuf, nkbuf, nrbuf, result, acc, peak, total,
     load_sem, out_sem, send_sem, recv_sem, q_send, q_recv, f_send, f_recv, r_send, r_recv,
 ):
-    pairs, groups, rows, width = codes_ref.shape
-    span = groups * rows
+    pairs, span, width = codes_ref.shape
+    groups = 4
+    rows = span // groups
     half = q_ref.shape[1]
     rope = qr_ref.shape[2]
+    blocks = scale_ref.shape[1]
     heads = half // new_ref.shape[1]
     fresh = new_ref.shape[1]
+    tail = groups * rope
     me = lax.axis_index("seq")
     inner = (me == 1) | (me == 2)
     outer = (me - 1) * 3
     across = 3 - me
     hub = 1 + me // 3
+    side = me // 2
 
     def neighbour_signal(target):
         pl.semaphore_signal(
@@ -131,25 +132,51 @@
             device_id_type=pl.DeviceIdType.MESH,
         )
 
-    loads = [
-        pltpu.make_async_copy(codes_ref, kbuf.at[0], load_sem.at[0]),
-        pltpu.make_async_copy(aux_ref, abuf.at[0], load_sem.at[1]),
-        pltpu.make_async_copy(q_ref, qbuf.at[:, 0], load_sem.at[2]),
-        pltpu.make_async_copy(qr_ref, qrbuf.at[:, 0], load_sem.at[3]),
-    ]
-    for load in loads:
-        load.start()
+    def load(c):
+        return (
+            pltpu.make_async_copy(codes_ref.at[c], raw.at[c], load_sem.at[0, c]),
+            pltpu.make_async_copy(rope_ref.at[c], rawr.at[c], load_sem.at[1, c]),
+            pltpu.make_async_copy(scale_ref.at[c], raws.at[c], load_sem.at[2, c]),
+            pltpu.make_async_copy(q_ref.at[c], qbuf.at[c, 0], load_sem.at[3, c]),
+            pltpu.make_async_copy(qr_ref.at[c], qrbuf.at[c, 0], load_sem.at[4, c]),
+        )
+
+    def start(copies):
+        for copy in copies:
+            copy.start()
+
+    for c in range(pairs):
+        start(load(c))
 
     @pl.when(inner)
     def _():
         neighbour_signal(outer)
         neighbour_signal(across)
-        pl.semaphore_wait(pltpu.get_barrier_semaphore(), 2)
 
     @pl.when(jnp.logical_not(inner))
     def _():
         neighbour_signal(hub)
-        pl.semaphore_wait(pltpu.get_barrier_semaphore(), 1)
+
+    def prepare(c):
+        for copy in load(c):
+            copy.wait()
+        for b in range(width // 128):
+            stage[b] = raw[c, :, b * 128:(b + 1) * 128].astype(jnp.float32)
+        for k in range(groups):
+            for b in range(width // 128):
+                kbuf[0, c, k // 2, (k % 2) * rows:(k % 2 + 1) * rows, b * 128:(b + 1) * 128] = (
+                    stage[b, pl.ds(k, rows, stride=groups), :].astype(jnp.bfloat16)
+                )
+        turned[...] = jnp.concatenate(
+            [rawr[c].astype(jnp.float32), raws[c].astype(jnp.float32),
+             jnp.zeros((128 - rope - blocks, span), jnp.float32)], axis=0
+        ).T
+        scales = []
+        for k in range(groups):
+            piece = turned[pl.ds(k, rows, stride=groups), :].T
+            abuf[0, c, k * rope:(k + 1) * rope, :] = piece[0:rope].astype(jnp.bfloat16)
+            scales.append(piece[rope:rope + blocks])
+        abuf[0, c, tail:, :] = jnp.concatenate(scales, axis=0).astype(jnp.bfloat16)
 
     def remote(src, dst, send, recv, target):
         return pltpu.make_async_remote_copy(
@@ -157,13 +184,22 @@
             device_id={"seq": target}, device_id_type=pl.DeviceIdType.MESH,
         )
 
-    def shard(src_slot, dst_slot, c, target):
+    def shard_head(src, dst, c, target, first):
         return (
-            remote(kbuf.at[src_slot, c], kbuf.at[dst_slot, c],
-                   send_sem.at[0, dst_slot, c], recv_sem.at[0, dst_slot, c], target),
-            remote(abuf.at[src_slot, c], abuf.at[dst_slot, c],
-                   send_sem.at[1, dst_slot, c], recv_sem.at[1, dst_slot, c], target),
-        )
+            remote(abuf.at[src, c], abuf.at[dst, c],
+                   send_sem.at[1, dst, c], recv_sem.at[1, dst, c], target),
+            remote(kbuf.at[src, c, first], kbuf.at[dst, c, first],
+                   send_sem.at[0, dst, c], recv_sem.at[0, dst, c], target),
+        )
+
+    def shard_rest(src, dst, c, target, first):
+        return (
+            remote(kbuf.at[src, c, 1 - first], kbuf.at[dst, c, 1 - first],
+                   send_sem.at[2, dst, c], recv_sem.at[2, dst, c], target),
+        )
+
+    def shard(src, dst, c, target, first):
+        return shard_head(src, dst, c, target, first) + shard_rest(src, dst, c, target, first)
 
     def queries(c, target):
         return (
@@ -175,71 +211,106 @@
         base = own + (slot % 2) * (partner - own)
         return base + (slot // 2) * (3 - 2 * base)
 
+    def key_part(slot, c, group):
+        return kbuf.at[slot, c, group // 2, pl.ds(pl.multiple_of((group % 2) * rows, rows), rows)]
+
+    def rope_part(slot, c, group):
+        return abuf.at[slot, c, pl.ds(pl.multiple_of(group * rope, rope), rope)]
+
+    def cache_part(c, place):
+        return cache_ref.at[c, pl.ds(pl.multiple_of(place * rows, rows), rows)]
+
+    def crope_part(c, place):
+        return crope_ref.at[c, :, pl.ds(pl.multiple_of(place * rows, rows), rows)]
+
     def handover(slot, c, group, place, target):
+        kept = slot + 1 - jnp.minimum(slot, 1)
         return (
-            remote(kbuf.at[slot, c, group], cache_ref.at[c, place],
+            remote(key_part(slot, c, group), cache_part(c, place),
                    f_send.at[0, slot, c], f_recv.at[0, slot, c], target),
-            remote(abuf.at[slot, c, group], caux_ref.at[c, place],
+            remote(rope_part(slot, c, group), crope_part(c, place),
                    f_send.at[1, slot, c], f_recv.at[1, slot, c], target),
+            remote(abuf.at[slot, c, pl.ds(tail, 16)], abuf.at[kept, c, pl.ds(tail, 16)],
+                   f_send.at[2, slot, c], f_recv.at[2, slot, c], target),
         )
 
     def keep(slot, c, place):
         return (
-            pltpu.make_async_copy(kbuf.at[slot, c, me], cache_ref.at[c, place], out_sem.at[0, slot, c]),
-            pltpu.make_async_copy(abuf.at[slot, c, me], caux_ref.at[c, place], out_sem.at[1, slot, c]),
-        )
+            pltpu.make_async_copy(key_part(slot, c, me), cache_part(c, place), out_sem.at[0, slot, c]),
+            pltpu.make_async_copy(rope_part(slot, c, me), crope_part(c, place), out_sem.at[1, slot, c]),
+        )
+
+    def keep_scales(slot, c, place):
+        tile = abuf[slot, c, tail:tail + 16, :].astype(jnp.float32)
+        mine = tile[0:blocks]
+        for k in range(1, groups):
+            mine = jnp.where(me == k, tile[k * blocks:(k + 1) * blocks], mine)
+        cscale_ref[c, :, pl.ds(pl.multiple_of(place * rows, rows), rows)] = mine.astype(jnp.bfloat16)
 
     def results(c, target):
         return remote(result.at[c], att_ref.at[c], r_send.at[c], r_recv.at[c], target)
 
-    def start(copies):
-        for copy in copies:
-            copy.start()
-
-    for load in loads:
-        load.wait()
+    prepare(0)
 
     @pl.when(jnp.logical_not(inner))
     def _():
+        pl.semaphore_wait(pltpu.get_barrier_semaphore(), 1)
+
         @pl.loop(0, pairs)
         def _(c):
-            copies = shard(0, 1, c, hub) + queries(c, hub)
+            copies = shard(0, 1, c, hub, side) + queries(c, hub)
             start(copies)
             start(keep(0, c, me))
+            keep_scales(0, c, me)
+
+            @pl.when(c + 1 < pairs)
+            def _():
+                prepare(c + 1)
+
             for copy in copies:
                 copy.wait_send()
 
         @pl.loop(0, pairs)
         def _(c):
             for slot in (0, 2, 3):
-                for copy in handover(slot, c, me, shard_of(slot, hub, me), hub):
+                place = shard_of(slot, hub, me)
+                for copy in handover(slot, c, me, place, hub):
                     copy.wait_recv()
+                keep_scales(max(slot, 1), c, place)
             results(c, hub).wait_recv()
             for copy in keep(0, c, me):
                 copy.wait()
 
     @pl.when(inner)
     def _():
-        start(shard(0, 2, 0, across))
-        start(shard(0, 2, 1, across))
+        pl.semaphore_wait(pltpu.get_barrier_semaphore(), 2)
 
         @pl.loop(0, pairs)
         def _(c):
+            @pl.when(c < 2)
+            def _():
+                start(shard(0, 2, c, across, 1 - side))
+
             start(handover(0, c, outer, me, outer))
             start(keep(0, c, me))
+            keep_scales(0, c, me)
             nkbuf[c] = jnp.zeros(nkbuf.shape[1:], nkbuf.dtype)
             nrbuf[c] = jnp.zeros(nrbuf.shape[1:], nrbuf.dtype)
             nkbuf[c, 0:fresh, :] = new_ref[c]
             nrbuf[c, 0:fresh, :] = newr_ref[c]
 
+            @pl.when(c + 1 < pairs)
+            def _():
+                prepare(c + 1)
+
         def relay(c):
-            for copy in shard(0, 1, c, outer):
+            for copy in shard(0, 1, c, outer, side):
                 copy.wait_recv()
-            start(shard(1, 3, c, across))
+            start(shard(1, 3, c, across, 1 - side))
             start(keep(1, c, outer))
 
         relay(0)
-        start(shard(0, 2, 2, across))
+        start(shard(0, 2, 2, across, 1 - side))
 
         @pl.loop(0, pairs)
         def _(c):
@@ -249,7 +320,7 @@
 
             @pl.when(c + 3 < pairs)
             def _():
-                start(shard(0, 2, c + 3, across))
+                start(shard(0, 2, c + 3, across, 1 - side))
 
             for copy in queries(c, outer):
                 copy.wait_recv()
@@ -270,35 +341,50 @@
             acc[...] = jnp.dot(w, nkbuf[c], preferred_element_type=jnp.float32)
             length = len_ref[c % len_ref.shape[0]]
 
-            @pl.loop(0, 4)
-            def _(slot):
+            @pl.loop(0, 8)
+            def _(step):
+                slot = step // 2
+                part = side + (step % 2) * (1 - 2 * side)
                 place = shard_of(slot, me, outer)
 
-                @pl.when(slot >= 2)
+                @pl.when((slot >= 2) & (step % 2 == 0))
                 def _():
-                    for copy in shard(0, slot, c, across):
+                    for copy in shard_head(0, slot, c, across, side):
                         copy.wait_recv()
                     start(handover(slot, c, outer, place, outer))
                     start(keep(slot, c, place))
 
-                keys, ropes = [], []
-                for k in range(groups):
-                    scales = abuf[slot, c, k, rope:AUX, :].astype(jnp.float32).T
-                    codes = kbuf[slot, c, k].astype(jnp.float32)
-                    blocks = [
-                        codes[:, b * 128:(b + 1) * 128] * scales[:, b:b + 1]
-                        for b in range(width // 128)
-                    ]
-                    keys.append(jnp.concatenate(blocks, axis=1).astype(jnp.bfloat16))
-                    ropes.append(abuf[slot, c, k, 0:rope, :])
+                @pl.when((slot >= 2) & (step % 2 == 1))
+                def _():
+                    for copy in shard_rest(0, slot, c, across, side):
+                        copy.wait_recv()
+
+                @pl.when((slot >= 1) & (step % 2 == 0))
+                def _():
+                    keep_scales(slot, c, place)
+
+                scales = abuf[slot, c, tail:tail + 16, :].astype(jnp.float32)
+                scales = jnp.where(side + step % 2 == 1, scales[8:16], scales[0:8]).T
+                keys = []
+                for k in range(2):
+                    codes = kbuf[slot, c, part, k * rows:(k + 1) * rows, :].astype(jnp.float32)
+                    keys.append(jnp.concatenate([
+                        codes[:, b * 128:(b + 1) * 128] * scales[:, k * blocks + b:k * blocks + b + 1]
+                        for b in range(blocks)
+                    ], axis=1).astype(jnp.bfloat16))
                 keys = jnp.concatenate(keys, axis=0)
+                base = pl.multiple_of(part * 2 * rope, 2 * rope)
+                ropes = jnp.concatenate(
+                    [abuf[slot, c, pl.ds(base, rope), :], abuf[slot, c, pl.ds(base + rope, rope), :]],
+                    axis=1,
+                )
                 q = qbuf[c].reshape(2 * half, width)
                 qr = qrbuf[c].reshape(2 * half, rope)
                 s = lax.dot_general(q, keys, dims, preferred_element_type=jnp.float32)
-                s = s + jnp.dot(qr, jnp.concatenate(ropes, axis=1), preferred_element_type=jnp.float32)
+                s = s + jnp.dot(qr, ropes, preferred_element_type=jnp.float32)
                 s = s * softmax_gain
-                column = lax.broadcasted_iota(jnp.int32, (1, span), 1)
-                position = place * span + (column % rows) * groups + column // rows
+                column = lax.broadcasted_iota(jnp.int32, (1, 2 * rows), 1)
+                position = place * span + (column % rows) * groups + 2 * part + column // rows
                 s = jnp.where(position < length, s, masked_score)
                 before = peak[:, 0:1]
                 m = jnp.maximum(before, jnp.max(s, axis=1, keepdims=True))
@@ -308,14 +394,13 @@
                 total[...] = factor * total[...] + jnp.sum(w.astype(jnp.float32), axis=1, keepdims=True)
                 acc[...] = factor * acc[...] + jnp.dot(w, keys, preferred_element_type=jnp.float32)
 
-            done = (acc[...] / total[:, 0:1]).astype(jnp.bfloat16)
-            result[c] = done[half:]
+            result[c] = (acc[half:, :] / total[half:, 0:1]).astype(jnp.bfloat16)
             results(c, outer).start()
-            att_ref[c] = done[:half]
+            att_ref[c] = (acc[:half, :] / total[:half, 0:1]).astype(jnp.bfloat16)
 
         @pl.loop(0, pairs)
         def _(c):
-            for copy in shard(0, 2, c, across) + shard(1, 3, c, across):
+            for copy in shard(0, 2, c, across, 1 - side) + shard(1, 3, c, across, 1 - side):
                 copy.wait_send()
             for slot in (0, 2, 3):
                 for copy in handover(slot, c, outer, shard_of(slot, me, outer), outer):
@@ -329,35 +414,35 @@
 def per_device_line(
     latent_codes, latent_scales, rope_keys, lengths, query_latent, query_rope, new_latent, new_rope
 ):
-    groups = 4
     layers, requests, span, width = latent_codes.shape
-    pairs, rows = layers * requests, span // groups
+    pairs, rows = layers * requests, span // 4
     rope, blocks = rope_keys.shape[-1], latent_scales.shape[-1]
     tokens, heads = query_latent.shape[2:4]
     half = tokens * heads
-    codes = latent_codes.reshape(pairs, rows, groups, width).transpose(0, 2, 1, 3)
-    ropes = rope_keys.reshape(pairs, rows, groups, rope).transpose(0, 2, 3, 1)
-    scales = latent_scales.reshape(pairs, rows, groups, blocks).transpose(0, 2, 3, 1)
-    aux = jnp.concatenate(
-        [ropes, scales, jnp.zeros((pairs, groups, AUX - rope - blocks, rows), jnp.bfloat16)], axis=2
-    )
+    aux = 4 * rope + 16
+    hbm_spec = pl.BlockSpec(memory_space=pltpu.HBM)
     any_spec = pl.BlockSpec(memory_space=pl.ANY)
     vmem_spec = pl.BlockSpec(memory_space=pltpu.VMEM)
     dma = pltpu.SemaphoreType.DMA
     bf16, f32 = jnp.bfloat16, jnp.float32
-    att, cache, caux = pl.pallas_call(
+    att, cache, crope, cscale = pl.pallas_call(
         _relay_kernel,
         out_shape=(
             jax.ShapeDtypeStruct((pairs, half, width), bf16),
-            jax.ShapeDtypeStruct((pairs, groups, rows, width), bf16),
-            jax.ShapeDtypeStruct((pairs, groups, AUX, rows), bf16),
+            jax.ShapeDtypeStruct((pairs, span, width), bf16),
+            jax.ShapeDtypeStruct((pairs, rope, span), bf16),
+            jax.ShapeDtypeStruct((pairs, blocks, span), bf16),
         ),
-        in_specs=[pl.BlockSpec(memory_space=pltpu.SMEM), any_spec, any_spec, any_spec, any_spec,
-                  vmem_spec, vmem_spec],
-        out_specs=(vmem_spec, any_spec, any_spec),
+        in_specs=[pl.BlockSpec(memory_space=pltpu.SMEM)] + [hbm_spec] * 5 + [vmem_spec] * 2,
+        out_specs=(vmem_spec, any_spec, any_spec, vmem_spec),
         scratch_shapes=[
-            pltpu.VMEM((4, pairs, groups, rows, width), bf16),
-            pltpu.VMEM((4, pairs, groups, AUX, rows), bf16),
+            pltpu.VMEM((4, pairs, 2, 2 * rows, width), bf16),
+            pltpu.VMEM((4, pairs, aux, rows), bf16),
+            pltpu.VMEM((pairs, span, width), bf16),
+            pltpu.VMEM((pairs, rope, span), bf16),
+            pltpu.VMEM((pairs, blocks, span), bf16),
+            pltpu.VMEM((width // 128, span, 128), f32),
+            pltpu.VMEM((span, 128), f32),
             pltpu.VMEM((pairs, 2, half, width), bf16),
             pltpu.VMEM((pairs, 2, half, rope), bf16),
             pltpu.VMEM((pairs, 128, width), bf16),
@@ -366,28 +451,30 @@
             pltpu.VMEM((2 * half, width), f32),
             pltpu.VMEM((2 * half, 128), f32),
             pltpu.VMEM((2 * half, 128), f32),
-            dma((4,)), dma((2, 4, pairs)), dma((2, 4, pairs)), dma((2, 4, pairs)),
-            dma((2, pairs)), dma((2, pairs)), dma((2, 4, pairs)), dma((2, 4, pairs)),
+            dma((5, pairs)), dma((2, 4, pairs)), dma((3, 4, pairs)), dma((3, 4, pairs)),
+            dma((2, pairs)), dma((2, pairs)), dma((3, 4, pairs)), dma((3, 4, pairs)),
             dma((pairs,)), dma((pairs,)),
         ],
         compiler_params=pltpu.CompilerParams(
             collective_id=0, has_side_effects=True, vmem_limit_bytes=40 << 20
         ),
     )(
-        lengths, codes, aux,
+        lengths, latent_codes.reshape(pairs, span, width),
+        rope_keys.transpose(0, 1, 3, 2).reshape(pairs, rope, span),
+        latent_scales.transpose(0, 1, 3, 2).reshape(pairs, blocks, span),
         query_latent.reshape(pairs, half, width), query_rope.reshape(pairs, half, rope),
         new_latent.reshape(pairs, tokens, width), new_rope.reshape(pairs, tokens, rope),
     )
-    spread = caux.reshape(layers, requests, groups, AUX, rows)
 
     def as_cache(values):
-        return values.transpose(0, 1, 2, 4, 3).reshape(layers, requests, span, 1, values.shape[3])
+        flipped = values.reshape(layers, requests, values.shape[1], span).transpose(0, 1, 3, 2)
+        return flipped.reshape(layers, requests, span, 1, values.shape[1])
 
     return (
         att.reshape(query_latent.shape),
         cache.reshape(layers, requests, span, 1, width),
-        as_cache(spread[:, :, :, rope:rope + blocks]),
-        as_cache(spread[:, :, :, :rope]),
+        as_cache(cscale),
+        as_cache(crope),
     )
 
 

time: 131 us -> 128 us (0.977)
  Pallas kernels: 119 us -> 117 us
    unnamed x13 -> x20, local copies, waits for them, and re-layouts: 3.91 us -> 10.7 us
    reshape x7 -> x0, local copies, waits for them, and re-layouts: 6.76 us -> none  [the longest x2 3.01 us: per_device_line(): latent_codes.reshape(pairs, rows, groups, width).transpose(0, 2, 1, 3)]
    pallas_call x1, Pallas kernels: 119 us -> 117 us  [per_device_line(): pl.pallas_call(_relay_kernel, out_shape=(jax.ShapeDtypeStruct((pairs, hal...]
where the time goes in v2:
time: 128 us
  Pallas kernels  117 us (91%)
  local copies, waits for them, and re-layouts  10.7 us (8%)
    pallas_call x1, Pallas kernels, per_device_line(): pl.pallas_call(_relay_kernel, out_shape=(jax.ShapeDtypeStruct((pairs, hal...  117 us
    unnamed x20, local copies, waits for them, and re-layouts  10.7 us

profile of v2, /device:TPU:0, one launch (start us, length us, event | category | flops | bytes accessed | tf_op | source)
XLA Modules:
  0.0 128.0 jit_solution(16650797441692763101)
XLA Ops:
  0.6 0.0 copy-start
  0.6 1.6 %copy-done = bf16[2,2,512,512]{3,2,1,0:T(8,128)(2,1)S(1)} copy-done((bf16[2,2,512,512]{3,2,1,0:T(8,128)(2,1)S(1)}, bf16[2,2,512,512]{3,2,1,0:T(8,128)(2,1)}, u32[]{:S(2)}) %copy-start) | copy-done | bytes 2097176
  2.2 0.0 copy-start.1
  2.2 1.0 copy-done.1
  3.3 0.0 copy-start.2
  3.3 0.9 copy-done.2
  4.2 0.0 copy-start.3
  4.2 0.9 copy-done.3
  5.1 0.0 copy-start.4
  5.1 0.7 copy-done.4
  5.8 0.0 copy-start.5
  5.8 0.7 copy-done.5
  6.6 0.0 copy-start.6
  6.6 0.7 copy-done.6
  7.2 0.0 copy-start.7
  7.2 0.7 copy-done.7
  7.9 116.6 %shard_map.111 = (bf16[4,128,512]{2,1,0:T(8,128)(2,1)S(1)}, bf16[4,512,512]{2,1,0:T(8,128)(2,1)S(1)}, bf16[4,64,512]{2,1,0:T(8,128)(2,1)S(1)}, bf16[4,4,512]{2,1,0:T(4,128)(2,1)S(1)}) custom-call(s32[2]{0:T(128)S(1)} %copy-done.7, bf16[4,512,512]{2,1,0:T(8,128)(2,1)S(1)} %bitcast.25, bf16[4,64,512]{2,1,0:T(8,128)(2,1)S(1)} %bitcast.29, ...), custom_call_target="tpu_custom_call" | custom-call | tf_op jit(solution)/shard_map/pallas_call | solution.py:428
  124.6 0.8 copy.17
  125.4 1.3 %copy.18 = bf16[2,2,512,1,512]{4,2,3,1,0:T(8,128)(2,1)} copy(bf16[2,2,512,1,512]{4,2,3,1,0:T(8,128)(2,1)S(1)} %bitcast.26) | data formatting | bytes 4194304
  126.7 0.6 copy.19
  127.3 0.7 copy.20
Async XLA Ops:
  0.6 1.6 %copy-start = (bf16[2,2,512,512]{3,2,1,0:T(8,128)(2,1)S(1)}, bf16[2,2,512,512]{3,2,1,0:T(8,128)(2,1)}, u32[]{:S(2)}) copy-start(bf16[2,2,512,512]{3,2,1,0:T(8,128)(2,1)} %param.8) | copy-start | bytes 6291460
  2.2 1.0 copy-start.1
  3.3 0.9 copy-start.2
  4.2 0.9 copy-start.3
  5.1 0.7 copy-start.4
  5.8 0.7 copy-start.5
  6.6 0.7 copy-start.6
  7.2 0.7 copy-start.7

commit v3 on v2

--- a/solution.py
+++ b/solution.py
@@ -456,7 +456,7 @@
             dma((pairs,)), dma((pairs,)),
         ],
         compiler_params=pltpu.CompilerParams(
-            collective_id=0, has_side_effects=True, vmem_limit_bytes=40 << 20
+            collective_id=0, has_side_effects=True, vmem_limit_bytes=60 << 20
         ),
     )(
         lengths, latent_codes.reshape(pairs, span, width),

time: 128 us -> 124 us (0.969)
  local copies, waits for them, and re-layouts: 10.7 us -> 6.28 us
    unnamed x20 -> x8, local copies, waits for them, and re-layouts: 10.7 us -> 6.28 us
where the time goes in v3:
time: 124 us; the launch traced here: 123 us
  Pallas kernels  116 us (94%)
  local copies, waits for them, and re-layouts  6.28 us (5%)
    pallas_call x1, Pallas kernels, per_device_line(): pl.pallas_call(_relay_kernel, out_shape=(jax.ShapeDtypeStruct((pairs, hal...  116 us
    unnamed x8, local copies, waits for them, and re-layouts  6.28 us

profile of v3, /device:TPU:0, one launch (start us, length us, event | category | flops | bytes accessed | tf_op | source)
XLA Modules:
  0.0 123.4 jit_solution(12942153514720326309)
XLA Ops:
  0.6 116.4 %shard_map.111 = (bf16[4,128,512]{2,1,0:T(8,128)(2,1)}, bf16[4,512,512]{2,1,0:T(8,128)(2,1)}, bf16[4,64,512]{2,1,0:T(8,128)(2,1)}, bf16[4,4,512]{2,1,0:T(4,128)(2,1)}) custom-call(s32[2]{0:T(128)} %len_ref.1, bf16[4,512,512]{2,1,0:T(8,128)(2,1)} %bitcast.25, bf16[4,64,512]{2,1,0:T(8,128)(2,1)} %bitcast.29, bf16[4,4,512]{2,1,0:T(4,128)(2,1)} %bitcast.32, ...), custom_call_target="tpu_custom_call" | custom-call | tf_op jit(solution)/shard_map/pallas_call | solution.py:428
  117.1 1.9 %copy.17 = bf16[2,2,4,32,512]{4,3,2,1,0:T(8,128)(2,1)} copy(bf16[2,2,4,32,512]{4,3,2,1,0:T(8,128)(2,1)} %bitcast.28) | data formatting | bytes 1048576
  119.0 0.0 copy-start.1
  119.0 0.0 copy-start
  119.0 3.1 %copy.18 = bf16[2,2,512,1,512]{4,2,3,1,0:T(8,128)(2,1)} copy(bf16[2,2,512,1,512]{4,2,3,1,0:T(8,128)(2,1)} %bitcast.26) | data formatting | bytes 4194304
  122.1 0.0 copy-done.1
  122.1 0.6 copy.19
  122.7 0.0 copy-done
  122.7 0.7 copy.20
Async XLA Ops:
  119.0 3.1 %copy-start.1 = (bf16[4,4,512]{2,1,0:T(4,128)(2,1)S(1)}, bf16[4,4,512]{2,1,0:T(4,128)(2,1)}, u32[]{:S(2)}) copy-start(bf16[4,4,512]{2,1,0:T(4,128)(2,1)} %get-tuple-element.10) | copy-start | bytes 49156
  119.0 3.7 %copy-start = (bf16[4,64,512]{2,1,0:T(8,128)(2,1)S(1)}, bf16[4,64,512]{2,1,0:T(8,128)(2,1)}, u32[]{:S(2)}) copy-start(bf16[4,64,512]{2,1,0:T(8,128)(2,1)} %get-tuple-element.11) | copy-start | bytes 786436

commit v4 on v3

--- a/solution.py
+++ b/solution.py
@@ -157,7 +157,7 @@
     def _():
         neighbour_signal(hub)
 
-    def prepare(c):
+    def prepare_codes(c):
         for copy in load(c):
             copy.wait()
         for b in range(width // 128):
@@ -167,6 +167,7 @@
                 kbuf[0, c, k // 2, (k % 2) * rows:(k % 2 + 1) * rows, b * 128:(b + 1) * 128] = (
                     stage[b, pl.ds(k, rows, stride=groups), :].astype(jnp.bfloat16)
                 )
+    def prepare_aux(c):
         turned[...] = jnp.concatenate(
             [rawr[c].astype(jnp.float32), raws[c].astype(jnp.float32),
              jnp.zeros((128 - rope - blocks, span), jnp.float32)], axis=0
@@ -178,19 +179,30 @@
             scales.append(piece[rope:rope + blocks])
         abuf[0, c, tail:, :] = jnp.concatenate(scales, axis=0).astype(jnp.bfloat16)
 
+    def prepare(c):
+        prepare_codes(c)
+        prepare_aux(c)
+
     def remote(src, dst, send, recv, target):
         return pltpu.make_async_remote_copy(
             src_ref=src, dst_ref=dst, send_sem=send, recv_sem=recv,
             device_id={"seq": target}, device_id_type=pl.DeviceIdType.MESH,
         )
 
-    def shard_head(src, dst, c, target, first):
+    def shard_aux(src, dst, c, target):
         return (
             remote(abuf.at[src, c], abuf.at[dst, c],
                    send_sem.at[1, dst, c], recv_sem.at[1, dst, c], target),
+        )
+
+    def shard_codes(src, dst, c, target, first):
+        return (
             remote(kbuf.at[src, c, first], kbuf.at[dst, c, first],
                    send_sem.at[0, dst, c], recv_sem.at[0, dst, c], target),
         )
+
+    def shard_head(src, dst, c, target, first):
+        return shard_aux(src, dst, c, target) + shard_codes(src, dst, c, target, first)
 
     def shard_rest(src, dst, c, target, first):
         return (
@@ -250,11 +262,13 @@
     def results(c, target):
         return remote(result.at[c], att_ref.at[c], r_send.at[c], r_recv.at[c], target)
 
-    prepare(0)
+    prepare_codes(0)
 
     @pl.when(jnp.logical_not(inner))
     def _():
         pl.semaphore_wait(pltpu.get_barrier_semaphore(), 1)
+
+        prepare_aux(0)
 
         @pl.loop(0, pairs)
         def _(c):
@@ -284,10 +298,13 @@
     @pl.when(inner)
     def _():
         pl.semaphore_wait(pltpu.get_barrier_semaphore(), 2)
+        start(shard_codes(0, 2, 0, across, 1 - side) + shard_rest(0, 2, 0, across, 1 - side))
+        prepare_aux(0)
+        start(shard_aux(0, 2, 0, across))
 
         @pl.loop(0, pairs)
         def _(c):
-            @pl.when(c < 2)
+            @pl.when(c == 1)
             def _():
                 start(shard(0, 2, c, across, 1 - side))
 

time: 124 us -> 124 us (level)
  no operation moved by 1% of the time
where the time goes in v4:
time: 124 us; the launch traced here: 123 us
  Pallas kernels  116 us (94%)
  local copies, waits for them, and re-layouts  6.28 us (5%)
    pallas_call x1, Pallas kernels, per_device_line(): pl.pallas_call(_relay_kernel, out_shape=(jax.ShapeDtypeStruct((pairs, hal...  116 us
    unnamed x8, local copies, waits for them, and re-layouts  6.28 us

profile of v4, /device:TPU:0, one launch (start us, length us, event | category | flops | bytes accessed | tf_op | source)
XLA Modules:
  0.0 123.3 jit_solution(9487150940174485189)
XLA Ops:
  0.6 116.3 %shard_map.111 = (bf16[4,128,512]{2,1,0:T(8,128)(2,1)}, bf16[4,512,512]{2,1,0:T(8,128)(2,1)}, bf16[4,64,512]{2,1,0:T(8,128)(2,1)}, bf16[4,4,512]{2,1,0:T(4,128)(2,1)}) custom-call(s32[2]{0:T(128)} %len_ref.1, bf16[4,512,512]{2,1,0:T(8,128)(2,1)} %bitcast.25, bf16[4,64,512]{2,1,0:T(8,128)(2,1)} %bitcast.29, bf16[4,4,512]{2,1,0:T(4,128)(2,1)} %bitcast.32, ...), custom_call_target="tpu_custom_call" | custom-call | tf_op jit(solution)/shard_map/pallas_call | solution.py:445
  117.0 1.9 %copy.17 = bf16[2,2,4,32,512]{4,3,2,1,0:T(8,128)(2,1)} copy(bf16[2,2,4,32,512]{4,3,2,1,0:T(8,128)(2,1)} %bitcast.28) | data formatting | bytes 1048576
  118.8 0.0 copy-start.1
  118.8 0.0 copy-start
  118.8 3.1 %copy.18 = bf16[2,2,512,1,512]{4,2,3,1,0:T(8,128)(2,1)} copy(bf16[2,2,512,1,512]{4,2,3,1,0:T(8,128)(2,1)} %bitcast.26) | data formatting | bytes 4194304
  121.9 0.0 copy-done.1
  121.9 0.6 copy.19
  122.5 0.0 copy-done
  122.5 0.7 copy.20
Async XLA Ops:
  118.8 3.1 %copy-start.1 = (bf16[4,4,512]{2,1,0:T(4,128)(2,1)S(1)}, bf16[4,4,512]{2,1,0:T(4,128)(2,1)}, u32[]{:S(2)}) copy-start(bf16[4,4,512]{2,1,0:T(4,128)(2,1)} %get-tuple-element.10) | copy-start | bytes 49156
  118.8 3.7 %copy-start = (bf16[4,64,512]{2,1,0:T(8,128)(2,1)S(1)}, bf16[4,64,512]{2,1,0:T(8,128)(2,1)}, u32[]{:S(2)}) copy-start(bf16[4,64,512]{2,1,0:T(8,128)(2,1)} %get-tuple-element.11) | copy-start | bytes 786436

commit v5 on v4

--- a/solution.py
+++ b/solution.py
@@ -260,7 +260,10 @@
         cscale_ref[c, :, pl.ds(pl.multiple_of(place * rows, rows), rows)] = mine.astype(jnp.bfloat16)
 
     def results(c, target):
-        return remote(result.at[c], att_ref.at[c], r_send.at[c], r_recv.at[c], target)
+        return remote(result.at[c, 1], att_ref.at[c], r_send.at[c], r_recv.at[c], target)
+
+    def own_results(c):
+        return pltpu.make_async_copy(result.at[c, 0], att_ref.at[c], load_sem.at[5, c])
 
     prepare_codes(0)
 
@@ -411,9 +414,10 @@
                 total[...] = factor * total[...] + jnp.sum(w.astype(jnp.float32), axis=1, keepdims=True)
                 acc[...] = factor * acc[...] + jnp.dot(w, keys, preferred_element_type=jnp.float32)
 
-            result[c] = (acc[half:, :] / total[half:, 0:1]).astype(jnp.bfloat16)
+            result[c, 1] = (acc[half:, :] / total[half:, 0:1]).astype(jnp.bfloat16)
             results(c, outer).start()
-            att_ref[c] = (acc[:half, :] / total[:half, 0:1]).astype(jnp.bfloat16)
+            result[c, 0] = (acc[:half, :] / total[:half, 0:1]).astype(jnp.bfloat16)
+            own_results(c).start()
 
         @pl.loop(0, pairs)
         def _(c):
@@ -426,6 +430,7 @@
                 for copy in keep(slot, c, shard_of(slot, me, outer)):
                     copy.wait()
             results(c, outer).wait_send()
+            own_results(c).wait()
 
 
 def per_device_line(
@@ -451,7 +456,7 @@
             jax.ShapeDtypeStruct((pairs, blocks, span), bf16),
         ),
         in_specs=[pl.BlockSpec(memory_space=pltpu.SMEM)] + [hbm_spec] * 5 + [vmem_spec] * 2,
-        out_specs=(vmem_spec, any_spec, any_spec, vmem_spec),
+        out_specs=(any_spec, any_spec, any_spec, vmem_spec),
         scratch_shapes=[
             pltpu.VMEM((4, pairs, 2, 2 * rows, width), bf16),
             pltpu.VMEM((4, pairs, aux, rows), bf16),
@@ -464,11 +469,11 @@
             pltpu.VMEM((pairs, 2, half, rope), bf16),
             pltpu.VMEM((pairs, 128, width), bf16),
             pltpu.VMEM((pairs, 128, rope), bf16),
-            pltpu.VMEM((pairs, half, width), bf16),
+            pltpu.VMEM((pairs, 2, half, width), bf16),
             pltpu.VMEM((2 * half, width), f32),
             pltpu.VMEM((2 * half, 128), f32),
             pltpu.VMEM((2 * half, 128), f32),
-            dma((5, pairs)), dma((2, 4, pairs)), dma((3, 4, pairs)), dma((3, 4, pairs)),
+            dma((6, pairs)), dma((2, 4, pairs)), dma((3, 4, pairs)), dma((3, 4, pairs)),
             dma((2, pairs)), dma((2, pairs)), dma((3, 4, pairs)), dma((3, 4, pairs)),
             dma((pairs,)), dma((pairs,)),
         ],

time: 124 us -> 123 us (level)
  no operation moved by 1% of the time
where the time goes in v5:
time: 123 us
  Pallas kernels  116 us (94%)
  local copies, waits for them, and re-layouts  6.28 us (5%)
    pallas_call x1, Pallas kernels, per_device_line(): pl.pallas_call(_relay_kernel, out_shape=(jax.ShapeDtypeStruct((pairs, hal...  116 us
    unnamed x8, local copies, waits for them, and re-layouts  6.28 us

profile of v5, /device:TPU:0, one launch (start us, length us, event | category | flops | bytes accessed | tf_op | source)
XLA Modules:
  0.0 123.2 jit_solution(6699092661879554664)
XLA Ops:
  0.6 116.3 %shard_map.111 = (bf16[4,128,512]{2,1,0:T(8,128)(2,1)}, bf16[4,512,512]{2,1,0:T(8,128)(2,1)}, bf16[4,64,512]{2,1,0:T(8,128)(2,1)}, bf16[4,4,512]{2,1,0:T(4,128)(2,1)}) custom-call(s32[2]{0:T(128)} %len_ref.1, bf16[4,512,512]{2,1,0:T(8,128)(2,1)} %bitcast.25, bf16[4,64,512]{2,1,0:T(8,128)(2,1)} %bitcast.29, bf16[4,4,512]{2,1,0:T(4,128)(2,1)} %bitcast.32, ...), custom_call_target="tpu_custom_call" | custom-call | tf_op jit(solution)/shard_map/pallas_call | solution.py:450
  116.9 1.9 %copy.17 = bf16[2,2,4,32,512]{4,3,2,1,0:T(8,128)(2,1)} copy(bf16[2,2,4,32,512]{4,3,2,1,0:T(8,128)(2,1)} %bitcast.28) | data formatting | bytes 1048576
  118.8 0.0 copy-start.1
  118.8 0.0 copy-start
  118.8 3.1 %copy.18 = bf16[2,2,512,1,512]{4,2,3,1,0:T(8,128)(2,1)} copy(bf16[2,2,512,1,512]{4,2,3,1,0:T(8,128)(2,1)} %bitcast.26) | data formatting | bytes 4194304
  121.9 0.0 copy-done.1
  121.9 0.6 copy.19
  122.5 0.0 copy-done
  122.5 0.7 copy.20
Async XLA Ops:
  118.8 3.1 %copy-start.1 = (bf16[4,4,512]{2,1,0:T(4,128)(2,1)S(1)}, bf16[4,4,512]{2,1,0:T(4,128)(2,1)}, u32[]{:S(2)}) copy-start(bf16[4,4,512]{2,1,0:T(4,128)(2,1)} %get-tuple-element.10) | copy-start | bytes 49156
  118.8 3.7 %copy-start = (bf16[4,64,512]{2,1,0:T(8,128)(2,1)S(1)}, bf16[4,64,512]{2,1,0:T(8,128)(2,1)}, u32[]{:S(2)}) copy-start(bf16[4,64,512]{2,1,0:T(8,128)(2,1)} %get-tuple-element.11) | copy-start | bytes 786436
